TPU v7x, 32 devices: a whole 2x2x4 slice. The times are simulated.
32 devices in a mesh: prompt: 8 (over y, x, core), seq: 4 (over z).
Axes of the slice: x: 2, y: 2, z: 4, core: 2. Of those that a mesh axis runs over, the one named last changes fastest.
Arguments:
- queries: bfloat16 [8, 512, 4096], P('prompt', 'seq'), may hold values from -8 to 8
- self_keys: bfloat16 [8, 512, 4096], P('prompt', 'seq'), may hold values from -8 to 8
- self_values: bfloat16 [8, 512, 4096], P('prompt', 'seq'), may hold values from -6 to 6
- cross_queries: bfloat16 [8, 512, 4096], P('prompt', 'seq')
- context: bfloat16 [8, 512, 5120], P('prompt', 'seq')
- key_weight: bfloat16 [5120, 4096], P('prompt', 'seq')
- value_weight: bfloat16 [5120, 4096], P('prompt', 'seq'), may hold values from -0.078125 to 0.078125
- lengths: int32 [8], P('prompt'), may hold values from 64 to 512, as said below
Outputs:
- attended: bfloat16 [8, 512, 4096], P('prompt', 'seq')
Inputs may be any that keep to these rules, and one draw needn't show every extreme that they name: `lengths`: each prompt's number of text tokens; some prompt has all 512.
All inputs are finite; a program needn't handle non-finite values.
Results may differ from a plain program's by a relative error of at most 0.007.
Values may be sent and summed in bfloat16 or wider, within the bound.
A program may use at most 128 MiB of HBM per device.

v0:
```python
import math

import jax
import jax.numpy as jnp
from jax import lax
from jax.sharding import PartitionSpec as P

HD = 128


def head_attend(query_rows, key_rows, value_rows, length, head_count):
    scaling = 1.0 / math.sqrt(HD)
    row_count = query_rows.shape[0]
    key_count = key_rows.shape[0]
    query_split = query_rows.reshape(row_count, head_count, HD)
    key_split = key_rows.reshape(key_count, head_count, HD)
    value_split = value_rows.reshape(key_count, head_count, HD)
    scores = (
        jnp.einsum("rhd,lhd->hrl", query_split, key_split, preferred_element_type=jnp.float32)
        * scaling
    )
    if length is None:
        row_max = jnp.max(scores, axis=2)
        weights = jnp.exp(scores - row_max[:, :, None])
    else:
        usable = (jnp.arange(key_count, dtype=jnp.int32) < length)[None, None, :]
        row_max = jnp.max(jnp.where(usable, scores, -jnp.inf), axis=2)
        shifted = jnp.where(usable, scores, row_max[:, :, None]) - row_max[:, :, None]
        weights = jnp.where(usable, jnp.exp(shifted), jnp.zeros_like(shifted))
    totals = jnp.sum(weights, axis=2)
    mixed = jnp.einsum(
        "hrl,lhd->rhd",
        weights.astype(jnp.bfloat16),
        value_split,
        preferred_element_type=jnp.float32,
    )
    return (
        (mixed / jnp.transpose(totals)[:, :, None])
        .reshape(row_count, head_count * HD)
        .astype(jnp.bfloat16)
    )


def by_blocks(function, query_rows):
    row_count = query_rows.shape[0]
    block_rows = math.gcd(row_count, 512)
    stacked = query_rows.reshape(row_count // block_rows, block_rows, query_rows.shape[1])
    return lax.map(function, stacked).reshape(row_count, -1)


def self_attend(query_heads, key_heads, value_heads, head_count):

    def self_run_block(block):
        return head_attend(block, key_heads, value_heads, None, head_count)

    return by_blocks(self_run_block, query_heads)


def cross_attend(query_rows, key_rows, value_rows, length, head_count):

    def cross_run_block(block):
        return head_attend(block, key_rows, value_rows, length, head_count)

    return by_blocks(cross_run_block, query_rows)


def body(
    queries, self_keys, self_values, cross_queries, context, key_weight, value_weight, lengths
):
    query_local = queries[0]
    key_local = self_keys[0]
    value_local = self_values[0]
    cross_local = cross_queries[0]
    length = lengths[0]
    head_local = key_weight.shape[1] // HD
    text_full = lax.all_gather(context[0], "seq", axis=0, tiled=True)
    key_sums = jnp.dot(
        text_full,
        lax.all_gather(key_weight, "prompt", axis=0, tiled=True),
        preferred_element_type=jnp.float32,
    )
    value_sums = jnp.dot(
        text_full,
        lax.all_gather(value_weight, "prompt", axis=0, tiled=True),
        preferred_element_type=jnp.float32,
    )
    text_keys = key_sums.astype(jnp.bfloat16)
    text_values = value_sums.astype(jnp.bfloat16)
    query_heads, key_heads, value_heads, cross_heads = (
        lax.all_to_all(query_local, "seq", split_axis=1, concat_axis=0, tiled=True),
        lax.all_to_all(key_local, "seq", split_axis=1, concat_axis=0, tiled=True),
        lax.all_to_all(value_local, "seq", split_axis=1, concat_axis=0, tiled=True),
        lax.all_to_all(cross_local, "seq", split_axis=1, concat_axis=0, tiled=True),
    )
    self_heads = self_attend(query_heads, key_heads, value_heads, head_local)
    cross_part = cross_attend(cross_heads, text_keys, text_values, length, head_local)
    summed = (self_heads.astype(jnp.float32) + cross_part.astype(jnp.float32)).astype(jnp.bfloat16)
    attended = lax.all_to_all(summed, "seq", split_axis=0, concat_axis=1, tiled=True)
    return attended[None]


def solution(mesh):
    in_specs = (
        P("prompt", "seq", None),
        P("prompt", "seq", None),
        P("prompt", "seq", None),
        P("prompt", "seq", None),
        P("prompt", "seq", None),
        P("prompt", "seq"),
        P("prompt", "seq"),
        P("prompt"),
    )
    out_specs = P("prompt", "seq", None)
    return jax.shard_map(body, mesh=mesh, in_specs=in_specs, out_specs=out_specs, check_vma=False)
```

profile of v0, /device:TPU:0, one launch (start us, length us, event | category | flops | bytes accessed | tf_op | source)
XLA Modules:
  0.0 361.7 jit_solution(14141983873178840253)
XLA Ops:
  6.5 0.7 all-gather.9.cloned.1.call-update
  8.7 1.9 all_to_all.58
  10.6 1.3 copy.28
  11.9 6.3 %all-to-all-start = ((bf16[128,4,1024]{2,0,1:T(8,128)(2,1)}), bf16[128,4,1024]{2,0,1:T(8,128)(2,1)S(1)}, u32[]{:S(2)}, u32[]{:S(2)}) async-start(bf16[128,4,1024]{2,0,1:T(8,128)(2,1)} %copy.28), calls=%async_computation | async-start | bytes 2097152 | tf_op jit(solution)/shard_map/all_to_all | solution.py:90
  18.2 0.8 all_to_all.61
  19.0 1.3 copy.29
  20.3 52.6 %all-to-all-done = bf16[128,4,1024]{2,0,1:T(8,128)(2,1)S(1)} async-done(((bf16[128,4,1024]{2,0,1:T(8,128)(2,1)}), bf16[128,4,1024]{2,0,1:T(8,128)(2,1)S(1)}, u32[]{:S(2)}, u32[]{:S(2)}) %all-to-all-start) | async-done | bytes 1048608 | tf_op jit(solution)/shard_map/all_to_all | solution.py:90
  72.9 3.5 all-to-all-start.1
  76.4 1.9 all_to_all.64
  78.3 1.3 copy.32
  79.6 46.6 %all-to-all-done.1 = bf16[128,4,1024]{2,0,1:T(8,128)(2,1)S(1)} async-done(((bf16[128,4,1024]{2,0,1:T(8,128)(2,1)}), bf16[128,4,1024]{2,0,1:T(8,128)(2,1)S(1)}, u32[]{:S(2)}, u32[]{:S(2)}) %all-to-all-start.1) | async-done | bytes 1048608 | tf_op jit(solution)/shard_map/all_to_all | solution.py:91
  126.2 7.5 %all-to-all-start.2 = ((bf16[128,4,1024]{2,0,1:T(8,128)(2,1)}), bf16[128,4,1024]{2,0,1:T(8,128)(2,1)S(1)}, u32[]{:S(2)}, u32[]{:S(2)}) async-start(bf16[128,4,1024]{2,0,1:T(8,128)(2,1)} %copy.32), calls=%async_computation.2 | async-start | bytes 2097152 | tf_op jit(solution)/shard_map/all_to_all | solution.py:92
  133.7 2.6 all_to_all.67
  136.3 2.5 copy.35
  138.9 32.6 %all-to-all-done.2 = bf16[128,4,1024]{2,0,1:T(8,128)(2,1)S(1)} async-done(((bf16[128,4,1024]{2,0,1:T(8,128)(2,1)}), bf16[128,4,1024]{2,0,1:T(8,128)(2,1)S(1)}, u32[]{:S(2)}, u32[]{:S(2)}) %all-to-all-start.2) | async-done | bytes 1048608 | tf_op jit(solution)/shard_map/all_to_all | solution.py:92
  171.5 4.4 %all-to-all-start.3 = ((bf16[128,4,1024]{2,0,1:T(8,128)(2,1)}), bf16[128,4,1024]{2,0,1:T(8,128)(2,1)}, u32[]{:S(2)}, u32[]{:S(2)}) async-start(bf16[128,4,1024]{2,0,1:T(8,128)(2,1)} %copy.35), calls=%async_computation.3 | async-start | bytes 2097152 | tf_op jit(solution)/shard_map/all_to_all | solution.py:93
  177.2 1.5 copy.51
  178.7 20.3 %all-to-all-done.3 = bf16[128,4,1024]{2,0,1:T(8,128)(2,1)} async-done(((bf16[128,4,1024]{2,0,1:T(8,128)(2,1)}), bf16[128,4,1024]{2,0,1:T(8,128)(2,1)}, u32[]{:S(2)}, u32[]{:S(2)}) %all-to-all-start.3) | async-done | bytes 1048608 | tf_op jit(solution)/shard_map/all_to_all | solution.py:93
  199.0 2.5 copy.52
  201.4 1.3 multiply_reduce_fusion
  202.7 3.5 copy-done
  206.3 1.4 fusion
  207.7 30.1 %all-gather.5.cloned.1.call-done = bf16[5120,1024]{1,0:T(8,128)(2,1)} async-done(((bf16[640,1024]{1,0:T(8,128)(2,1)}), bf16[5120,1024]{1,0:T(8,128)(2,1)}) %all-gather.5.cloned.1.call-update) | async-done | bytes 10485776 | tf_op jit(solution)/shard_map/all_gather | solution.py:84
  237.8 9.8 %fusion.16 = bf16[512,1024]{1,0:T(8,128)(2,1)S(1)} fusion(bf16[5120,1024]{1,0:T(8,128)(2,1)} %all-gather.5.cloned.1.call-done, bf16[1,512,5120]{2,1,0:T(8,128)(2,1)} %all-gather.9.cloned.1.call-done), kind=kOutput, calls=%fused_computation.22 | convolution fusion | flops 5369233408 | bytes 16777216 | tf_op jit(solution)/shard_map/dot_general | solution.py:82
  248.2 54.7 %all-gather.7.cloned.1.call-done = bf16[5120,1024]{1,0:T(8,128)(2,1)} async-done(((bf16[640,1024]{1,0:T(8,128)(2,1)}), bf16[5120,1024]{1,0:T(8,128)(2,1)}) %all-gather.7.cloned.1.call-update) | async-done | bytes 10485776 | tf_op jit(solution)/shard_map/all_gather | solution.py:79
  302.8 9.8 %fusion.22 = bf16[64,8,8,128]{3,2,1,0:T(8,128)(2,1)S(1)} fusion(bf16[5120,1024]{1,0:T(8,128)(2,1)} %all-gather.7.cloned.1.call-done, bf16[1,512,5120]{2,1,0:T(8,128)(2,1)} %all-gather.9.cloned.1.call-done), kind=kOutput, calls=%fused_computation.24 | convolution fusion | flops 5369233408 | bytes 16777216 | tf_op jit(solution)/shard_map/dot_general | solution.py:77
  312.7 1.3 select_reduce_fusion
  314.0 2.4 bitcast_reduce_fusion
  316.5 2.5 fusion.12
  319.0 2.5 add_convert_fusion
  322.7 30.5 %all_to_all.77 = bf16[4,128,1024]{2,1,0:T(8,128)(2,1)S(1)} all-to-all(bf16[4,128,1024]{2,1,0:T(8,128)(2,1)S(1)} %convert_element_type.54), channel_id=1, replica_groups=mesh['prompt'=8,'seq'=4] {'seq'}, dimensions={0} | all-to-all | bytes 2097152 | tf_op jit(solution)/shard_map/all_to_all | solution.py:98
  353.9 1.3 copy.43
  (25 shorter events, 4.4 us)
Async XLA Ops:
  6.5 11.7 %copy-start.2 = (bf16[1,128,4096]{2,1,0:T(8,128)(2,1)S(1)}, bf16[1,128,4096]{2,1,0:T(8,128)(2,1)}, u32[]{:S(2)}) copy-start(bf16[1,128,4096]{2,1,0:T(8,128)(2,1)} %param.9) | copy-start | bytes 3145732
  6.5 201.1 %all-gather.9.cloned.1.call-start = ((), (), s32[]{:S(2)}) async-start(), calls=%async_computation.7 | async-start | bytes 6553600 | tf_op jit(solution)/shard_map/all_gather | solution.py:76
  7.3 230.5 %all-gather.5.cloned.1.call-start = ((), (), s32[]{:S(2)}) async-start(), calls=%async_computation.5 | async-start | bytes 11796480 | tf_op jit(solution)/shard_map/all_gather | solution.py:84
  8.0 294.8 %all-gather.7.cloned.1.call-start = ((), (), s32[]{:S(2)}) async-start(), calls=%async_computation.6 | async-start | bytes 11796480 | tf_op jit(solution)/shard_map/all_gather | solution.py:79
  11.9 61.0 %all-to-all-start = ((bf16[128,4,1024]{2,0,1:T(8,128)(2,1)}), bf16[128,4,1024]{2,0,1:T(8,128)(2,1)S(1)}, u32[]{:S(2)}, u32[]{:S(2)}) async-start(bf16[128,4,1024]{2,0,1:T(8,128)(2,1)} %copy.28), calls=%async_computation | async-start | bytes 2097152 | tf_op jit(solution)/shard_map/all_to_all | solution.py:90
  72.9 53.3 %all-to-all-start.1 = ((bf16[128,4,1024]{2,0,1:T(8,128)(2,1)}), bf16[128,4,1024]{2,0,1:T(8,128)(2,1)S(1)}, u32[]{:S(2)}, u32[]{:S(2)}) async-start(bf16[128,4,1024]{2,0,1:T(8,128)(2,1)} %copy.29), calls=%async_computation.1 | async-start | bytes 2097152 | tf_op jit(solution)/shard_map/all_to_all | solution.py:91
  126.2 45.3 %all-to-all-start.2 = ((bf16[128,4,1024]{2,0,1:T(8,128)(2,1)}), bf16[128,4,1024]{2,0,1:T(8,128)(2,1)S(1)}, u32[]{:S(2)}, u32[]{:S(2)}) async-start(bf16[128,4,1024]{2,0,1:T(8,128)(2,1)} %copy.32), calls=%async_computation.2 | async-start | bytes 2097152 | tf_op jit(solution)/shard_map/all_to_all | solution.py:92
  171.5 5.1 %copy-start.1 = (bf16[128,4,1024]{2,0,1:T(8,128)(2,1)}, bf16[128,4,1024]{2,0,1:T(8,128)(2,1)S(1)}, u32[]{:S(2)}) copy-start(bf16[128,4,1024]{2,0,1:T(8,128)(2,1)S(1)} %all-to-all-done.2) | copy-start | bytes 3145732
  171.5 27.5 %all-to-all-start.3 = ((bf16[128,4,1024]{2,0,1:T(8,128)(2,1)}), bf16[128,4,1024]{2,0,1:T(8,128)(2,1)}, u32[]{:S(2)}, u32[]{:S(2)}) async-start(bf16[128,4,1024]{2,0,1:T(8,128)(2,1)} %copy.35), calls=%async_computation.3 | async-start | bytes 2097152 | tf_op jit(solution)/shard_map/all_to_all | solution.py:93
  202.7 3.5 copy-start
  248.2 64.5 %copy-start.3 = (bf16[64,8,8,128]{3,2,1,0:T(8,128)(2,1)S(1)}, bf16[64,8,8,128]{3,2,1,0:T(8,128)(2,1)}, u32[]{:S(2)}) copy-start(bf16[64,8,8,128]{3,2,1,0:T(8,128)(2,1)} %copy.52) | copy-start | bytes 3145732
  314.0 5.0 %slice-start = ((s8[8388608]{0:T(1024)(128)(4,1)}), s8[4194304]{0:T(1024)(128)(4,1)S(1)}, s32[]{:S(2)}) async-start(s8[8388608]{0:T(1024)(128)(4,1)} %bitcast.60), calls=%async_computation.8 | async-start | bytes 8388608
  316.5 2.5 slice-start.1
Sparse Core Ops, SparseCore 0:
  8.9 164.6 all-gather.8
  175.5 62.2 all-gather.4
  239.7 63.1 all-gather.6
where the time goes:
time: 362 us
  waiting for transfers between devices  239 us (66%)
  blocking collectives  30.5 us (8%)
  matrix products  27.2 us (8%)
  local copies, waits for them, and re-layouts  25.3 us (7%)
  starting transfers between devices  21.9 us (6%)
  between operations  14 us (4%)
  other arithmetic  3.83 us (1%)
    all_gather x1, waiting for transfers between devices, body(): lax.all_gather(key_weight, 'prompt', axis=0, tiled=True)  54.7 us
    all_to_all x1, waiting for transfers between devices, body(): lax.all_to_all(query_local, 'seq', split_axis=1, concat_axis=0, tiled=True)  52.6 us
    all_to_all x1, waiting for transfers between devices, body(): lax.all_to_all(key_local, 'seq', split_axis=1, concat_axis=0, tiled=True)  46.6 us
    all_to_all x1, waiting for transfers between devices, body(): lax.all_to_all(value_local, 'seq', split_axis=1, concat_axis=0, tiled=True)  32.6 us
    all_to_all x1, blocking collectives, body(): lax.all_to_all(summed, 'seq', split_axis=0, concat_axis=1, tiled=True)  30.5 us
    all_gather x1, waiting for transfers between devices, body(): lax.all_gather(value_weight, 'prompt', axis=0, tiled=True)  30.1 us
    all_to_all x1, waiting for transfers between devices, body(): lax.all_to_all(cross_local, 'seq', split_axis=1, concat_axis=0, tiled=True)  20.3 us
    dot_general x1, matrix products, body(): jnp.dot(text_full, lax.all_gather(key_weight, 'prompt', axis=0, tiled=Tru...  9.82 us
  transfers between devices with their start and end apart: 7, of which 6 were waited for; matrix products, arithmetic and copies ran while one was open for 7% of the time, Pallas kernels for 0%

commit v1 on v0

v1 whole, which is shorter than its diff:
```python
import functools
import math

import jax
import jax.numpy as jnp
from jax import lax
from jax.experimental import pallas as pl
from jax.experimental.pallas import tpu as pltpu
from jax.sharding import PartitionSpec as P

HD = 128
CORES = 2
Q, K, V, CTX, CQ = range(5)


def kernel(
    seq_size,
    prompt_size,
    length_ref,
    q_hbm,
    k_hbm,
    v_hbm,
    cq_hbm,
    ctx_hbm,
    wk_hbm,
    wv_hbm,
    out_hbm,
    q_buf,
    k_buf,
    v_buf,
    cq_buf,
    ctx_buf,
    wk_buf,
    wv_buf,
    text_keys,
    text_values,
    self_buf,
    out_buf,
    local_sem,
    seq_send,
    seq_recv,
    chip_send,
    chip_recv,
    pair_send,
    pair_recv,
    out_send,
    out_recv,
):
    seq = lax.axis_index("seq")
    prompt = lax.axis_index("prompt")
    chips = prompt_size // CORES
    chip = prompt // CORES
    core = prompt % CORES
    partner = chip * CORES + (1 - core)
    tokens = q_hbm.shape[0]
    width = wk_hbm.shape[1]
    depth = wk_hbm.shape[0]
    heads = width // HD
    scaling = 1.0 / math.sqrt(HD)

    def seq_peer(offset):
        return lax.rem(seq + offset, seq_size)

    def seq_source(offset):
        return lax.rem(seq + seq_size - offset, seq_size)

    def chip_peer(offset):
        return lax.rem(chip + offset, chips) * CORES + core

    def chip_source(offset):
        return lax.rem(chip + chips - offset, chips) * CORES + core

    barrier = pltpu.get_barrier_semaphore()
    for offset in range(1, seq_size):
        pl.semaphore_signal(
            barrier, inc=1, device_id={"seq": seq_peer(offset)}, device_id_type=pl.DeviceIdType.MESH
        )
    for offset in range(1, chips):
        pl.semaphore_signal(
            barrier,
            inc=1,
            device_id={"prompt": chip_peer(offset)},
            device_id_type=pl.DeviceIdType.MESH,
        )
    pl.semaphore_signal(
        barrier, inc=1, device_id={"prompt": partner}, device_id_type=pl.DeviceIdType.MESH
    )
    pl.semaphore_wait(barrier, seq_size - 1 + chips - 1 + 1)

    def token_rows(owner):
        return pl.ds(pl.multiple_of(owner * tokens, tokens), tokens)

    def text_rows(owner):
        text = ctx_hbm.shape[0]
        return pl.ds(pl.multiple_of(owner * text, text), text)

    def head_columns(owner):
        return pl.ds(pl.multiple_of(owner * width, width), width)

    def weight_rows(owner):
        return pl.ds(pl.multiple_of(owner * depth, depth), depth)

    sources = {Q: q_hbm, K: k_hbm, V: v_hbm, CTX: ctx_hbm, CQ: cq_hbm}
    buffers = {Q: q_buf, K: k_buf, V: v_buf, CTX: ctx_buf, CQ: cq_buf}

    def piece(which, owner):
        if which == CTX:
            return sources[which]
        return sources[which].at[:, head_columns(owner)]

    def landing(which, owner):
        rows = text_rows(owner) if which == CTX else token_rows(owner)
        return buffers[which].at[rows]

    def seq_copy(which, offset):
        return pltpu.make_async_remote_copy(
            src_ref=piece(which, seq_peer(offset)),
            dst_ref=landing(which, seq),
            send_sem=seq_send.at[which, offset],
            recv_sem=seq_recv.at[which, offset],
            device_id={"seq": seq_peer(offset)},
            device_id_type=pl.DeviceIdType.MESH,
        )

    weights = ((wk_hbm, wk_buf), (wv_hbm, wv_buf))

    def chip_copy(which, offset):
        shard, gathered = weights[which]
        return pltpu.make_async_remote_copy(
            src_ref=shard,
            dst_ref=gathered.at[weight_rows(prompt)],
            send_sem=chip_send.at[which, offset],
            recv_sem=chip_recv.at[which, offset],
            device_id={"prompt": chip_peer(offset)},
            device_id_type=pl.DeviceIdType.MESH,
        )

    def pair_copy(which, offset):
        shard, gathered = weights[which]
        rows = weight_rows(chip_source(offset))
        return pltpu.make_async_remote_copy(
            src_ref=shard if offset == 0 else gathered.at[rows],
            dst_ref=gathered.at[rows],
            send_sem=pair_send.at[which, offset],
            recv_sem=pair_recv.at[which, offset],
            device_id={"prompt": partner},
            device_id_type=pl.DeviceIdType.MESH,
        )

    def out_copy(offset):
        return pltpu.make_async_remote_copy(
            src_ref=out_buf.at[token_rows(seq_source(offset))],
            dst_ref=out_hbm.at[:, head_columns(seq)],
            send_sem=out_send.at[offset],
            recv_sem=out_recv.at[offset],
            device_id={"seq": seq_source(offset)},
            device_id_type=pl.DeviceIdType.MESH,
        )

    offsets = range(1, seq_size)
    for which in (Q, K, V):
        for offset in offsets:
            seq_copy(which, offset).start()
    for which in range(2):
        for offset in range(1, chips):
            chip_copy(which, offset).start()
    for which in (CTX, CQ):
        for offset in offsets:
            seq_copy(which, offset).start()
    local_copies = [
        pltpu.make_async_copy(
            piece(which, seq), landing(which, seq), local_sem.at[which]
        )
        for which in (Q, K, V, CTX, CQ)
    ] + [
        pltpu.make_async_copy(
            weights[which][0], weights[which][1].at[weight_rows(prompt)], local_sem.at[5 + which]
        )
        for which in range(2)
    ]
    for copy in local_copies:
        copy.start()
    for which in range(2):
        pair_copy(which, 0).start()
    for copy in local_copies:
        copy.wait()

    def head_attend(query, key, value, length):
        scores = lax.dot_general(
            query, key, (((1,), (1,)), ((), ())), preferred_element_type=jnp.float32
        )
        if length is not None:
            slot = lax.broadcasted_iota(jnp.int32, scores.shape, 1)
            scores = jnp.where(slot < length, scores, -jnp.inf)
        row_max = jnp.max(scores, axis=1, keepdims=True)
        exps = jnp.exp((scores - row_max) * scaling)
        totals = jnp.sum(exps, axis=1, keepdims=True)
        mixed = jnp.dot(exps.astype(jnp.bfloat16), value, preferred_element_type=jnp.float32)
        return (mixed / totals).astype(jnp.bfloat16)

    def forward(which):
        for offset in range(1, chips):
            chip_copy(which, offset).wait_recv()
            pair_copy(which, offset).start()

    forward(0)
    for which in (Q, K, V):
        for offset in offsets:
            seq_copy(which, offset).wait_recv()

    def self_head(head, carry):
        columns = pl.ds(pl.multiple_of(head * HD, HD), HD)
        key = k_buf[:, columns]
        value = v_buf[:, columns]

        def block(index, inner):
            rows = token_rows(index)
            self_buf[rows, columns] = head_attend(q_buf[rows, columns], key, value, None)
            return inner

        return lax.fori_loop(0, seq_size, block, carry)

    lax.fori_loop(0, heads, self_head, 0)

    forward(1)
    for offset in offsets:
        seq_copy(CTX, offset).wait_recv()

    def project(which, target):
        for offset in range(chips):
            pair_copy(which, offset).wait_recv()
        gathered = weights[which][1]
        tile = math.gcd(width, 256)

        def column_tile(index, carry):
            columns = pl.ds(pl.multiple_of(index * tile, tile), tile)
            target[:, columns] = jnp.dot(
                ctx_buf[...], gathered[:, columns], preferred_element_type=jnp.float32
            ).astype(jnp.bfloat16)
            return carry

        lax.fori_loop(0, width // tile, column_tile, 0)

    project(0, text_keys)
    project(1, text_values)
    length = length_ref[0]

    for offset in tuple(offsets) + (0,):
        if offset:
            seq_copy(CQ, offset).wait_recv()
        rows = token_rows(seq_source(offset))

        def cross_head(head, carry):
            columns = pl.ds(pl.multiple_of(head * HD, HD), HD)
            part = head_attend(
                cq_buf[rows, columns], text_keys[:, columns], text_values[:, columns], length
            )
            out_buf[rows, columns] = (
                self_buf[rows, columns].astype(jnp.float32) + part.astype(jnp.float32)
            ).astype(jnp.bfloat16)
            return carry

        lax.fori_loop(0, heads, cross_head, 0)
        if offset:
            out_copy(offset).start()
    own = pltpu.make_async_copy(
        out_buf.at[token_rows(seq)], out_hbm.at[:, head_columns(seq)], local_sem.at[7]
    )
    own.start()

    for which in (Q, K, V, CTX, CQ):
        for offset in offsets:
            seq_copy(which, offset).wait_send()
    for which in range(2):
        for offset in range(1, chips):
            chip_copy(which, offset).wait_send()
        for offset in range(chips):
            pair_copy(which, offset).wait_send()
    own.wait()
    for offset in offsets:
        out_copy(offset).wait()


def body(
    seq_size,
    prompt_size,
    queries,
    self_keys,
    self_values,
    cross_queries,
    context,
    key_weight,
    value_weight,
    lengths,
):
    tokens = queries.shape[1]
    full = tokens * seq_size
    width = key_weight.shape[1]
    model = context.shape[2]
    chips = prompt_size // CORES
    text_full = context.shape[1] * seq_size
    activations = pltpu.VMEM((full, width), jnp.bfloat16)
    texts = pltpu.VMEM((text_full, width), jnp.bfloat16)
    dma = pltpu.SemaphoreType.DMA
    attended = pl.pallas_call(
        functools.partial(kernel, seq_size, prompt_size),
        out_shape=jax.ShapeDtypeStruct(queries.shape[1:], jnp.bfloat16),
        in_specs=[pl.BlockSpec(memory_space=pltpu.SMEM)]
        + [pl.BlockSpec(memory_space=pl.ANY)] * 7,
        out_specs=pl.BlockSpec(memory_space=pl.ANY),
        scratch_shapes=[activations] * 4
        + [pltpu.VMEM((text_full, model), jnp.bfloat16)]
        + [pltpu.VMEM((model, width), jnp.bfloat16)] * 2
        + [texts] * 2
        + [activations] * 2
        + [
            dma((8,)),
            dma((5, seq_size)),
            dma((5, seq_size)),
            dma((2, chips)),
            dma((2, chips)),
            dma((2, chips)),
            dma((2, chips)),
            dma((seq_size,)),
            dma((seq_size,)),
        ],
        compiler_params=pltpu.CompilerParams(
            collective_id=0, has_side_effects=True, vmem_limit_bytes=60 * 1024 * 1024
        ),
    )(
        lengths,
        queries[0],
        self_keys[0],
        self_values[0],
        cross_queries[0],
        context[0],
        key_weight,
        value_weight,
    )
    return attended[None]


def solution(mesh):
    in_specs = (
        P("prompt", "seq", None),
        P("prompt", "seq", None),
        P("prompt", "seq", None),
        P("prompt", "seq", None),
        P("prompt", "seq", None),
        P("prompt", "seq"),
        P("prompt", "seq"),
        P("prompt"),
    )
    out_specs = P("prompt", "seq", None)
    step = functools.partial(body, mesh.shape["seq"], mesh.shape["prompt"])
    return jax.shard_map(step, mesh=mesh, in_specs=in_specs, out_specs=out_specs, check_vma=False)
```

time: 362 us -> 242 us (0.67)
  Pallas kernels: 0 us -> 239 us
  waiting for transfers between devices: 239 us -> 0 us
  blocking collectives: 30.5 us -> 0 us
  matrix products: 27.2 us -> 0 us
  local copies, waits for them, and re-layouts: 25.3 us -> 2.29 us
  starting transfers between devices: 21.9 us -> 0 us
  between operations: 14 us -> 0.66 us
  other arithmetic: 3.83 us -> 0 us
    pallas_call x0 -> x1, Pallas kernels: none -> 239 us  [body(): pl.pallas_call(functools.partial(kernel, seq_size, prompt_size), out_shap...]
    all_to_all x4 -> x0, waiting for transfers between devices: 152 us -> none  [the longest x1 52.6 us: body(): lax.all_to_all(query_local, 'seq', split_axis=1, concat_axis=0, tiled=True)]
    all_gather x3 -> x0, waiting for transfers between devices: 84.8 us -> none  [the longest x1 54.7 us: body(): lax.all_gather(key_weight, 'prompt', axis=0, tiled=True)]
    all_to_all x1 -> x0, blocking collectives: 30.5 us -> none  [body(): lax.all_to_all(summed, 'seq', split_axis=0, concat_axis=1, tiled=True)]
    dot_general x6 -> x0, matrix products: 27.2 us -> none  [the longest x1 9.82 us: body(): jnp.dot(text_full, lax.all_gather(key_weight, 'prompt', axis=0, tiled=Tru...]
    all_to_all x4 -> x0, starting transfers between devices: 21.8 us -> none  [the longest x1 7.5 us: body(): lax.all_to_all(value_local, 'seq', split_axis=1, concat_axis=0, tiled=True)]
    all_to_all x9 -> x0, local copies, waits for them, and re-layouts: 14.2 us -> none  [the longest x2 5.14 us: body(): lax.all_to_all(cross_local, 'seq', split_axis=1, concat_axis=0, tiled=True)]
    unnamed x16 -> x1, local copies, waits for them, and re-layouts: 8.07 us -> 2.29 us
  transfers between devices with their start and end apart: 7 -> 0, of which waited for: 6 -> 0; matrix products, arithmetic and copies ran while one was open for 7% -> 0% of each run, Pallas kernels for 0% -> 0%
where the time goes in v1:
time: 242 us
  Pallas kernels  239 us (99%)
    pallas_call x1, Pallas kernels, body(): pl.pallas_call(functools.partial(kernel, seq_size, prompt_size), out_shap...  239 us

profile of v1, /device:TPU:0, one launch (start us, length us, event | category | flops | bytes accessed | tf_op | source)
XLA Modules:
  0.0 242.0 jit_solution(442841828193645765)
XLA Ops:
  0.7 239.1 %shard_map.82 = bf16[128,4096]{1,0:T(8,128)(2,1)} custom-call(s32[1]{0:T(128)S(6)} %copy.10.length_ref, bf16[128,4096]{1,0:T(8,128)(2,1)} %bitcast.8, bf16[128,4096]{1,0:T(8,128)(2,1)} %bitcast.9, bf16[128,4096]{1,0:T(8,128)(2,1)} %bitcast.10, bf16[128,4096]{1,0:T(8,128)(2,1)} %bitcast.11, bf16[128,5120]{1,0:T(8,128)(2,1)} %bitcast.7, ...), custom_call_target="tpu_custom_call" | custom-call | tf_op jit(solution)/shard_map/pallas_call | solution.py:305
  239.7 2.3 copy.11

commit v2 on v1

--- a/solution.py
+++ b/solution.py
@@ -34,11 +34,12 @@
     wv_buf,
     text_keys,
     text_values,
-    self_buf,
     out_buf,
     local_sem,
     seq_send,
     seq_recv,
+    text_send,
+    text_recv,
     chip_send,
     chip_recv,
     pair_send,
@@ -122,6 +123,41 @@
             device_id_type=pl.DeviceIdType.MESH,
         )
 
+    def text_start_here(way, hop):
+        if way == 0:
+            return (seq >= hop) & (seq + 1 < seq_size)
+        return (seq + hop < seq_size) & (seq >= 1)
+
+    def text_lands_here(way, hop):
+        return seq >= hop + 1 if way == 0 else seq + 1 + hop < seq_size
+
+    def text_copy(way, hop):
+        owner = seq - hop if way == 0 else seq + hop
+        peer = seq_peer(1 if way == 0 else seq_size - 1)
+        rows = text_rows(owner)
+        return pltpu.make_async_remote_copy(
+            src_ref=ctx_hbm if hop == 0 else ctx_buf.at[rows],
+            dst_ref=ctx_buf.at[rows],
+            send_sem=text_send.at[way, hop],
+            recv_sem=text_recv.at[way, hop],
+            device_id={"seq": peer},
+            device_id_type=pl.DeviceIdType.MESH,
+        )
+
+    def start_text(hop):
+        for way in range(2):
+
+            @pl.when(text_start_here(way, hop))
+            def _():
+                text_copy(way, hop).start()
+
+    def wait_text(hop):
+        for way in range(2):
+
+            @pl.when(text_lands_here(way, hop))
+            def _():
+                text_copy(way, hop).wait_recv()
+
     weights = ((wk_hbm, wk_buf), (wv_hbm, wv_buf))
 
     def chip_copy(which, offset):
@@ -158,15 +194,18 @@
         )
 
     offsets = range(1, seq_size)
-    for which in (Q, K, V):
+
+    def start_pieces(*group):
         for offset in offsets:
-            seq_copy(which, offset).start()
+            for which in group:
+                seq_copy(which, offset).start()
+
+    groups = [(K,), (V,), (Q, CQ)]
+    start_text(0)
+    start_pieces(*groups[0])
     for which in range(2):
         for offset in range(1, chips):
             chip_copy(which, offset).start()
-    for which in (CTX, CQ):
-        for offset in offsets:
-            seq_copy(which, offset).start()
     local_copies = [
         pltpu.make_async_copy(
             piece(which, seq), landing(which, seq), local_sem.at[which]
@@ -203,28 +242,17 @@
             chip_copy(which, offset).wait_recv()
             pair_copy(which, offset).start()
 
-    forward(0)
-    for which in (Q, K, V):
-        for offset in offsets:
-            seq_copy(which, offset).wait_recv()
-
-    def self_head(head, carry):
-        columns = pl.ds(pl.multiple_of(head * HD, HD), HD)
-        key = k_buf[:, columns]
-        value = v_buf[:, columns]
-
-        def block(index, inner):
-            rows = token_rows(index)
-            self_buf[rows, columns] = head_attend(q_buf[rows, columns], key, value, None)
-            return inner
-
-        return lax.fori_loop(0, seq_size, block, carry)
-
-    lax.fori_loop(0, heads, self_head, 0)
-
-    forward(1)
-    for offset in offsets:
-        seq_copy(CTX, offset).wait_recv()
+    hops = seq_size - 1
+    for hop in range(hops):
+        wait_text(hop)
+        if hop + 1 < hops:
+            start_text(hop + 1)
+        if hop + 1 < len(groups):
+            start_pieces(*groups[hop + 1])
+        if hop == 0:
+            forward(0)
+    for group in groups[max(hops, 1) :]:
+        start_pieces(*group)
 
     def project(which, target):
         for offset in range(chips):
@@ -242,25 +270,31 @@
         lax.fori_loop(0, width // tile, column_tile, 0)
 
     project(0, text_keys)
+    forward(1)
     project(1, text_values)
+    for which in (K, V):
+        for offset in offsets:
+            seq_copy(which, offset).wait_recv()
     length = length_ref[0]
 
-    for offset in tuple(offsets) + (0,):
+    for offset in range(seq_size):
         if offset:
+            seq_copy(Q, offset).wait_recv()
             seq_copy(CQ, offset).wait_recv()
         rows = token_rows(seq_source(offset))
 
-        def cross_head(head, carry):
+        def head_block(head, carry):
             columns = pl.ds(pl.multiple_of(head * HD, HD), HD)
+            alone = head_attend(q_buf[rows, columns], k_buf[:, columns], v_buf[:, columns], None)
             part = head_attend(
                 cq_buf[rows, columns], text_keys[:, columns], text_values[:, columns], length
             )
             out_buf[rows, columns] = (
-                self_buf[rows, columns].astype(jnp.float32) + part.astype(jnp.float32)
+                alone.astype(jnp.float32) + part.astype(jnp.float32)
             ).astype(jnp.bfloat16)
             return carry
 
-        lax.fori_loop(0, heads, cross_head, 0)
+        lax.fori_loop(0, heads, head_block, 0)
         if offset:
             out_copy(offset).start()
     own = pltpu.make_async_copy(
@@ -268,9 +302,16 @@
     )
     own.start()
 
-    for which in (Q, K, V, CTX, CQ):
+    for which in (Q, K, V, CQ):
         for offset in offsets:
             seq_copy(which, offset).wait_send()
+    for hop in range(hops):
+        for way in range(2):
+
+            @pl.when(text_start_here(way, hop))
+            def _():
+                text_copy(way, hop).wait_send()
+
     for which in range(2):
         for offset in range(1, chips):
             chip_copy(which, offset).wait_send()
@@ -312,11 +353,13 @@
         + [pltpu.VMEM((text_full, model), jnp.bfloat16)]
         + [pltpu.VMEM((model, width), jnp.bfloat16)] * 2
         + [texts] * 2
-        + [activations] * 2
+        + [activations]
         + [
             dma((8,)),
             dma((5, seq_size)),
             dma((5, seq_size)),
+            dma((2, seq_size)),
+            dma((2, seq_size)),
             dma((2, chips)),
             dma((2, chips)),
             dma((2, chips)),

time: 242 us -> 221 us (0.913)
  Pallas kernels: 239 us -> 218 us
    pallas_call x1, Pallas kernels: 239 us -> 218 us  [body(): pl.pallas_call(functools.partial(kernel, seq_size, prompt_size), out_shap...]
where the time goes in v2:
time: 221 us
  Pallas kernels  218 us (99%)
  local copies, waits for them, and re-layouts  2.29 us (1%)
    pallas_call x1, Pallas kernels, body(): pl.pallas_call(functools.partial(kernel, seq_size, prompt_size), out_shap...  218 us

profile of v2, /device:TPU:0, one launch (start us, length us, event | category | flops | bytes accessed | tf_op | source)
XLA Modules:
  0.0 220.5 jit_solution(4873129438290304195)
XLA Ops:
  0.7 217.6 %shard_map.82 = bf16[128,4096]{1,0:T(8,128)(2,1)} custom-call(s32[1]{0:T(128)S(6)} %copy.10.length_ref, bf16[128,4096]{1,0:T(8,128)(2,1)} %bitcast.8, bf16[128,4096]{1,0:T(8,128)(2,1)} %bitcast.9, bf16[128,4096]{1,0:T(8,128)(2,1)} %bitcast.10, bf16[128,4096]{1,0:T(8,128)(2,1)} %bitcast.11, bf16[128,5120]{1,0:T(8,128)(2,1)} %bitcast.7, ...), custom_call_target="tpu_custom_call" | custom-call | tf_op jit(solution)/shard_map/pallas_call | solution.py:346
  218.3 2.3 %copy.11 = bf16[1,128,4096]{2,1,0:T(8,128)(2,1)} copy(bf16[1,128,4096]{2,1,0:T(8,128)(2,1)} %bitcast.6) | data formatting | bytes 2097152

commit v3 on v2

--- a/solution.py
+++ b/solution.py
@@ -200,9 +200,10 @@
             for which in group:
                 seq_copy(which, offset).start()
 
-    groups = [(K,), (V,), (Q, CQ)]
+    groups = [[], [], [(K,), (V,), (Q, CQ)]]
     start_text(0)
-    start_pieces(*groups[0])
+    for group in groups[0]:
+        start_pieces(*group)
     for which in range(2):
         for offset in range(1, chips):
             chip_copy(which, offset).start()
@@ -247,11 +248,11 @@
         wait_text(hop)
         if hop + 1 < hops:
             start_text(hop + 1)
-        if hop + 1 < len(groups):
-            start_pieces(*groups[hop + 1])
-        if hop == 0:
+        for group in sum(groups[hop + 1 : hop + 2], []):
+            start_pieces(*group)
+        if hop == min(1, hops - 1):
             forward(0)
-    for group in groups[max(hops, 1) :]:
+    for group in sum(groups[hops + 1 :], []):
         start_pieces(*group)
 
     def project(which, target):

time: 221 us -> 200 us (0.905)
  Pallas kernels: 218 us -> 197 us
    pallas_call x1, Pallas kernels: 218 us -> 197 us  [body(): pl.pallas_call(functools.partial(kernel, seq_size, prompt_size), out_shap...]
where the time goes in v3:
time: 200 us
  Pallas kernels  197 us (98%)
  local copies, waits for them, and re-layouts  2.29 us (1%)
    pallas_call x1, Pallas kernels, body(): pl.pallas_call(functools.partial(kernel, seq_size, prompt_size), out_shap...  197 us

profile of v3, /device:TPU:0, one launch (start us, length us, event | category | flops | bytes accessed | tf_op | source)
XLA Modules:
  0.0 200.1 jit_solution(1438989716322783666)
XLA Ops:
  0.7 197.2 %shard_map.82 = bf16[128,4096]{1,0:T(8,128)(2,1)} custom-call(s32[1]{0:T(128)S(6)} %copy.10.length_ref, bf16[128,4096]{1,0:T(8,128)(2,1)} %bitcast.8, bf16[128,4096]{1,0:T(8,128)(2,1)} %bitcast.9, bf16[128,4096]{1,0:T(8,128)(2,1)} %bitcast.10, bf16[128,4096]{1,0:T(8,128)(2,1)} %bitcast.11, bf16[128,5120]{1,0:T(8,128)(2,1)} %bitcast.7, ...), custom_call_target="tpu_custom_call" | custom-call | tf_op jit(solution)/shard_map/pallas_call | solution.py:347
  197.8 2.3 %copy.11 = bf16[1,128,4096]{2,1,0:T(8,128)(2,1)} copy(bf16[1,128,4096]{2,1,0:T(8,128)(2,1)} %bitcast.6) | data formatting | bytes 2097152

commit v4 on v3

--- a/solution.py
+++ b/solution.py
@@ -34,6 +34,7 @@
     wv_buf,
     text_keys,
     text_values,
+    self_buf,
     out_buf,
     local_sem,
     seq_send,
@@ -196,11 +197,11 @@
     offsets = range(1, seq_size)
 
     def start_pieces(*group):
-        for offset in offsets:
+        for offset in sorted(offsets, key=lambda offset: abs(2 * offset - seq_size)):
             for which in group:
                 seq_copy(which, offset).start()
 
-    groups = [[], [], [(K,), (V,), (Q, CQ)]]
+    groups = [[], [], [(K,), (V,), (Q,), (CQ,)]]
     start_text(0)
     for group in groups[0]:
         start_pieces(*group)
@@ -273,20 +274,34 @@
     project(0, text_keys)
     forward(1)
     project(1, text_values)
-    for which in (K, V):
+    for which in (K, V, Q):
         for offset in offsets:
             seq_copy(which, offset).wait_recv()
+
+    def self_head(head, carry):
+        columns = pl.ds(pl.multiple_of(head * HD, HD), HD)
+        key = k_buf[:, columns]
+        value = v_buf[:, columns]
+
+        def block(index, inner):
+            rows = token_rows(index)
+            self_buf[rows, columns] = head_attend(q_buf[rows, columns], key, value, None)
+            return inner
+
+        return lax.fori_loop(0, seq_size, block, carry)
+
+    lax.fori_loop(0, heads, self_head, 0)
     length = length_ref[0]
 
-    for offset in range(seq_size):
+    arrival = sorted(offsets, key=lambda offset: abs(2 * offset - seq_size))
+    for offset in arrival + [0]:
         if offset:
-            seq_copy(Q, offset).wait_recv()
             seq_copy(CQ, offset).wait_recv()
         rows = token_rows(seq_source(offset))
 
         def head_block(head, carry):
             columns = pl.ds(pl.multiple_of(head * HD, HD), HD)
-            alone = head_attend(q_buf[rows, columns], k_buf[:, columns], v_buf[:, columns], None)
+            alone = self_buf[rows, columns]
             part = head_attend(
                 cq_buf[rows, columns], text_keys[:, columns], text_values[:, columns], length
             )
@@ -354,7 +369,7 @@
         + [pltpu.VMEM((text_full, model), jnp.bfloat16)]
         + [pltpu.VMEM((model, width), jnp.bfloat16)] * 2
         + [texts] * 2
-        + [activations]
+        + [activations] * 2
         + [
             dma((8,)),
             dma((5, seq_size)),

time: 200 us -> 194 us (0.970)
  Pallas kernels: 197 us -> 191 us
    pallas_call x1, Pallas kernels: 197 us -> 191 us  [body(): pl.pallas_call(functools.partial(kernel, seq_size, prompt_size), out_shap...]
where the time goes in v4:
time: 194 us
  Pallas kernels  191 us (98%)
  local copies, waits for them, and re-layouts  2.29 us (1%)
    pallas_call x1, Pallas kernels, body(): pl.pallas_call(functools.partial(kernel, seq_size, prompt_size), out_shap...  191 us

profile of v4, /device:TPU:0, one launch (start us, length us, event | category | flops | bytes accessed | tf_op | source)
XLA Modules:
  0.0 193.6 jit_solution(8250778357503916404)
XLA Ops:
  0.7 190.6 %shard_map.82 = bf16[128,4096]{1,0:T(8,128)(2,1)} custom-call(s32[1]{0:T(128)S(6)} %copy.10.length_ref, bf16[128,4096]{1,0:T(8,128)(2,1)} %bitcast.8, bf16[128,4096]{1,0:T(8,128)(2,1)} %bitcast.9, bf16[128,4096]{1,0:T(8,128)(2,1)} %bitcast.10, bf16[128,4096]{1,0:T(8,128)(2,1)} %bitcast.11, bf16[128,5120]{1,0:T(8,128)(2,1)} %bitcast.7, ...), custom_call_target="tpu_custom_call" | custom-call | tf_op jit(solution)/shard_map/pallas_call | solution.py:362
  191.3 2.3 %copy.11 = bf16[1,128,4096]{2,1,0:T(8,128)(2,1)} copy(bf16[1,128,4096]{2,1,0:T(8,128)(2,1)} %bitcast.6) | data formatting | bytes 2097152
